TPU v7x, 128 devices: a whole 4x4x4 slice. The times are simulated.
128 devices in a mesh: grp: 8 (over y, core), wide: 16 (over z, x).
Axes of the slice: x: 4, y: 4, z: 4, core: 2. Of those that a mesh axis runs over, the one named last changes fastest.
Arguments:
- coefficients: bfloat16 [2048, 2, 128, 512], P(('grp', 'wide')), may hold values from -6 to 6
- source_blocks: bfloat16 [2, 2048, 2, 128, 256], P(None, ('grp', 'wide')), may hold values from -0.25 to 0.25
- target_blocks: bfloat16 [3, 2048, 2, 128, 256], P(None, ('grp', 'wide')), may hold values from -0.25 to 0.25
- pair_tables: int32 [2, 128, 16], P(None, ('grp', 'wide')), may hold values from 0 to 15, each once within a row
Outputs:
- target_coeffs: bfloat16 [2048, 2, 128, 512], P(('grp', 'wide'))
Inputs may be any that keep to these rules, and one draw needn't show every extreme that they name: Each row pair_tables[s, d] is a permutation of the numbers 0 to 15.
All inputs are finite; a program needn't handle non-finite values.
Results may differ from a plain program's by a relative error of at most 0.007.
Values may be sent and summed in bfloat16 or wider, within the bound.
No kernel may reach another device: no remote copies, remote signals or barrier semaphores. Data moves between devices by JAX's collectives and lax.ppermute only.
A program may use at most 128 MiB of HBM per device.

v0:
```python
import jax
import jax.numpy as jnp
from jax import lax
from jax.sharding import PartitionSpec as P


def swapped(value, axis, distance):
    mask = 2**distance
    pairs = [(source, source ^ mask) for source in range(lax.axis_size(axis))]
    return lax.ppermute(value, axis, pairs)


def complex_terms(blocks, stacked):
    real_part = jnp.einsum(
        "nij,njk->nik", blocks[:, 0], stacked[:, 0], preferred_element_type=jnp.float32
    ) - jnp.einsum("nij,njk->nik", blocks[:, 1], stacked[:, 1], preferred_element_type=jnp.float32)
    imag_part = jnp.einsum(
        "nij,njk->nik", blocks[:, 0], stacked[:, 1], preferred_element_type=jnp.float32
    ) + jnp.einsum("nij,njk->nik", blocks[:, 1], stacked[:, 0], preferred_element_type=jnp.float32)
    return jnp.stack([real_part, imag_part], axis=1)


def source_level(local_boxes, local_blocks, order_row):
    picked = jnp.take(local_boxes, order_row, axis=0)
    count = picked.shape[0]
    paired = picked.reshape((count // 2, 2) + picked.shape[1:])
    joined = jnp.concatenate([paired[:, 0], paired[:, 1]], axis=2)
    joined = jnp.repeat(joined, 2, axis=0)
    return complex_terms(local_blocks, joined).astype(jnp.bfloat16)


def target_levels(state, target_blocks):
    bit_count = lax.axis_size("grp").bit_length() - 1
    group_id = lax.axis_index("grp")
    for layer_idx in range(target_blocks.shape[0]):
        bit_num = layer_idx % bit_count
        partner = swapped(state, "grp", bit_num)
        is_upper = group_id >> bit_num & 1 == 1
        level_blocks = target_blocks[layer_idx]
        lower_part = jnp.where(is_upper, partner, state)
        upper_part = jnp.where(is_upper, state, partner)
        joined = jnp.concatenate([lower_part, upper_part], axis=2)
        state = complex_terms(level_blocks, joined).astype(jnp.bfloat16)
    return state


def on_device(coefficients, source_blocks, target_blocks, pair_tables):
    current = coefficients
    for layer_idx in range(source_blocks.shape[0]):
        current = source_level(current, source_blocks[layer_idx], pair_tables[layer_idx, 0])
    current = lax.all_to_all(current, "wide", split_axis=0, concat_axis=0, tiled=True)
    return target_levels(current, target_blocks)


def solution(mesh):
    in_specs = (
        P(("grp", "wide"), None, None, None),
        P(None, ("grp", "wide"), None, None, None),
        P(None, ("grp", "wide"), None, None, None),
        P(None, ("grp", "wide"), None),
    )
    out_specs = P(("grp", "wide"), None, None, None)
    return jax.shard_map(
        on_device, mesh=mesh, in_specs=in_specs, out_specs=out_specs, check_vma=False
    )
```

profile of v0, /device:TPU:0, one launch (start us, length us, event | category | flops | bytes accessed | tf_op | source)
XLA Modules:
  0.0 362.2 jit_solution(13352660391859560353)
XLA Ops:
  0.7 5.0 %gather_fusion = bf16[16,2,128,512]{3,2,1,0:T(8,128)(2,1)} fusion(bf16[16,2,128,512]{3,2,1,0:T(8,128)(2,1)} %param.6, s32[1024]{0:T(1024)S(1)} %get-tuple-element.28), kind=kCustom, calls=%fused_computation.clone | custom fusion | bytes 8388672 | tf_op jit(solution)/shard_map/jit(_take)/gather | solution.py:24
  5.7 2.6 broadcast_select_fusion.1
  8.8 2.4 pad_maximum_fusion.3
  11.2 6.3 %copy.24 = bf16[8,2,256,512]{2,3,0,1:T(8,128)(2,1)} copy(bf16[8,2,256,512]{3,2,1,0:T(8,128)(2,1)} %pad_maximum_fusion.3) | data formatting | bytes 8388608 | tf_op jit(solution)/shard_map/concatenate | solution.py:27
  17.5 2.7 fusion.55
  20.6 6.4 %broadcast_in_dim.15 = bf16[8,2,2,256,512]{3,4,1,0,2:T(8,128)(2,1)} broadcast(bf16[8,2,256,512]{2,3,0,1:T(8,128)(2,1)} %copy.24), dimensions={0,2,3,4} | broadcast | bytes 12582912 | tf_op jit(solution)/shard_map/broadcast_in_dim | solution.py:28
  27.0 3.6 fusion.10
  35.4 2.4 pad_maximum_fusion.4
  37.8 5.2 %gather_fusion.1 = bf16[16,2,128,512]{2,3,1,0:T(8,128)(2,1)} fusion(bf16[16,2,128,512]{2,3,0,1:T(8,128)(2,1)} %pad_maximum_fusion.4, s32[1024]{0:T(1024)S(1)} %get-tuple-element.27), kind=kCustom, calls=%fused_computation.1.clone | custom fusion | bytes 8388672 | tf_op jit(solution)/shard_map/jit(_take)/gather | solution.py:24
  43.0 2.6 broadcast_select_fusion
  46.7 2.3 copy.27
  49.0 6.4 %broadcast_in_dim.16 = bf16[8,2,2,256,512]{3,4,1,0,2:T(8,128)(2,1)} broadcast(bf16[8,2,256,512]{2,3,0,1:T(8,128)(2,1)} %copy.27), dimensions={0,2,3,4} | broadcast | bytes 12582912 | tf_op jit(solution)/shard_map/broadcast_in_dim | solution.py:28
  55.4 3.6 fusion.14
  64.9 58.8 %all_to_all.5 = bf16[16,2,128,512]{2,3,1,0:T(8,128)(2,1)} all-to-all(bf16[16,2,128,512]{2,3,1,0:T(8,128)(2,1)S(1)} %copy.29), channel_id=1, replica_groups=mesh['grp'=8,'wide'=16] {'wide'}, dimensions={0} | all-to-all | bytes 8388608 | tf_op jit(solution)/shard_map/all_to_all | solution.py:51
  123.7 6.2 %copy.30 = bf16[16,2,128,512]{3,2,0,1:T(8,128)(2,1)} copy(bf16[16,2,128,512]{2,3,1,0:T(8,128)(2,1)} %all_to_all.5) | data formatting | bytes 8388608 | tf_op jit(solution)/shard_map/all_to_all | solution.py:51
  129.9 5.7 %fusion.54 = (bf16[1,16,2,128,256]{4,3,2,1,0:T(8,128)(2,1)S(1)}, bf16[1,16,2,128,256]{4,3,2,1,0:T(8,128)(2,1)}, bf16[1,16,2,128,256]{4,3,2,1,0:T(8,128)(2,1)}) fusion(bf16[3,16,2,128,256]{4,3,2,1,0:T(8,128)(2,1)} %param.8), kind=kLoop, calls=%fused_computation.107 | loop fusion | bytes 12582912 | tf_op jit(solution)/shard_map/slice | solution.py:39
  137.7 2.5 broadcast_select_fusion.2
  144.4 2.6 pad_maximum_fusion.7
  148.5 1.9 copy.59
  150.4 89.9 %collective-permute-done.1 = bf16[16,2,128,512]{3,2,0,1:T(8,128)(2,1)} collective-permute-done((bf16[16,2,128,512]{3,2,0,1:T(8,128)(2,1)}, bf16[16,2,128,512]{3,2,0,1:T(8,128)(2,1)}, u32[]{:S(2)}, u32[]{:S(2)}) %collective-permute-start.1) | collective-permute-done | bytes 4194336 | tf_op jit(solution)/shard_map/ppermute | solution.py:10
  240.3 2.5 broadcast_select_fusion.4
  246.9 2.6 pad_maximum_fusion.8
  249.5 3.2 collective-permute-start.2
  252.7 1.9 copy.57
  254.6 88.9 %collective-permute-done.2 = bf16[16,2,128,512]{3,2,0,1:T(8,128)(2,1)} collective-permute-done((bf16[16,2,128,512]{3,2,0,1:T(8,128)(2,1)}, bf16[16,2,128,512]{3,2,0,1:T(8,128)(2,1)}, u32[]{:S(2)}, u32[]{:S(2)}) %collective-permute-start.2) | collective-permute-done | bytes 4194336 | tf_op jit(solution)/shard_map/ppermute | solution.py:10
  343.5 2.5 broadcast_select_fusion.6
  346.0 1.7 fusion.35
  347.7 2.1 fusion.34
  349.9 1.8 fusion.23
  351.7 1.8 fusion.26
  353.5 2.3 pad_maximum_fusion.9
  355.8 6.4 %copy.40 = bf16[16,2,128,512]{3,2,1,0:T(8,128)(2,1)} copy(bf16[16,2,128,512]{2,3,0,1:T(8,128)(2,1)} %pad_maximum_fusion.9) | data formatting | bytes 8388608 | tf_op jit(solution)/shard_map/stack | solution.py:20
  (40 shorter events, 25.2 us)
Async XLA Ops:
  27.0 4.6 %copy-start.1 = (bf16[8,2,2,256,512]{3,4,1,0,2:T(8,128)(2,1)S(1)}, bf16[8,2,2,256,512]{3,4,1,0,2:T(8,128)(2,1)}, u32[]{:S(2)}) copy-start(bf16[8,2,2,256,512]{3,4,1,0,2:T(8,128)(2,1)} %broadcast_in_dim.15) | copy-start | bytes 25165828
  55.4 4.6 %copy-start = (bf16[8,2,2,256,512]{3,4,1,0,2:T(8,128)(2,1)S(1)}, bf16[8,2,2,256,512]{3,4,1,0,2:T(8,128)(2,1)}, u32[]{:S(2)}) copy-start(bf16[8,2,2,256,512]{3,4,1,0,2:T(8,128)(2,1)} %broadcast_in_dim.16) | copy-start | bytes 25165828
  129.9 7.5 %collective-permute-start = (bf16[16,2,128,512]{3,2,0,1:T(8,128)(2,1)}, bf16[16,2,128,512]{3,2,0,1:T(8,128)(2,1)}, u32[]{:S(2)}, u32[]{:S(2)}) collective-permute-start(bf16[16,2,128,512]{3,2,0,1:T(8,128)(2,1)} %copy.30), channel_id=1, source_target_pairs={{0,16},{16,0},{32,48},{48,32},{64,80},{80,64},{96,112},{112,96},{1... | collective-permute-start | bytes 12582920 | tf_op jit(solution)/shard_map/ppermute | solution.py:10
  135.5 2.2 copy-start.6
  144.3 2.6 copy-start.4
  146.9 93.3 %collective-permute-start.1 = (bf16[16,2,128,512]{3,2,0,1:T(8,128)(2,1)}, bf16[16,2,128,512]{3,2,0,1:T(8,128)(2,1)}, u32[]{:S(2)}, u32[]{:S(2)}) collective-permute-start(bf16[16,2,128,512]{3,2,0,1:T(8,128)(2,1)} %pad_maximum_fusion.7), channel_id=1, source_target_pairs={{0,32},{16,48},{32,0},{48,16},{64,96},{80,112},{96,64},{112,80},{1... | collective-permute-start | bytes 12582920 | tf_op jit(solution)/shard_map/ppermute | solution.py:10
  148.5 91.7 %copy-start.5 = (bf16[16,1,128,512]{3,2,0,1:T(8,128)(2,1)S(1)}, bf16[16,1,128,512]{3,2,0,1:T(8,128)(2,1)}, u32[]{:S(2)}) copy-start(bf16[16,1,128,512]{3,2,0,1:T(8,128)(2,1)} %copy-done.4) | copy-start | bytes 6291460
  246.9 2.6 copy-start.2
  249.5 94.0 %collective-permute-start.2 = (bf16[16,2,128,512]{3,2,0,1:T(8,128)(2,1)}, bf16[16,2,128,512]{3,2,0,1:T(8,128)(2,1)}, u32[]{:S(2)}, u32[]{:S(2)}) collective-permute-start(bf16[16,2,128,512]{3,2,0,1:T(8,128)(2,1)} %pad_maximum_fusion.8), channel_id=1, source_target_pairs={{0,64},{16,80},{32,96},{48,112},{64,0},{80,16},{96,32},{112,48},{1... | collective-permute-start | bytes 12582920 | tf_op jit(solution)/shard_map/ppermute | solution.py:10
  252.7 90.8 %copy-start.3 = (bf16[16,1,128,512]{3,2,0,1:T(8,128)(2,1)S(1)}, bf16[16,1,128,512]{3,2,0,1:T(8,128)(2,1)}, u32[]{:S(2)}) copy-start(bf16[16,1,128,512]{3,2,0,1:T(8,128)(2,1)} %copy-done.2) | copy-start | bytes 6291460
where the time goes:
time: 363 us; the launch traced here: 362 us
  waiting for transfers between devices  180 us (50%)
  local copies, waits for them, and re-layouts  60.6 us (17%)
  blocking collectives  58.8 us (16%)
  matrix products  30.6 us (8%)
  other arithmetic  26.8 us (7%)
  starting transfers between devices  4.77 us (1%)
    ppermute x3, waiting for transfers between devices, swapped(): return lax.ppermute(value, axis, pairs)  180 us
    all_to_all x1, blocking collectives, on_device(): lax.all_to_all(current, 'wide', split_axis=0, concat_axis=0, tiled=True)  58.8 us
    broadcast_in_dim x2, local copies, waits for them, and re-layouts, source_level(): joined = jnp.repeat(joined, 2, axis=0)  12.7 us
    dot_general x5, matrix products, complex_terms(): jnp.einsum('nij,njk->nik', blocks[:, 0], stacked[:, 0], preferred_element...  10.9 us
    another operation x5, other arithmetic, complex_terms(): return jnp.stack([real_part, imag_part], axis=1)  10.3 us
    gather x2, local copies, waits for them, and re-layouts, source_level(): picked = jnp.take(local_boxes, order_row, axis=0)  10.2 us
    concatenate x2, local copies, waits for them, and re-layouts, source_level(): joined = jnp.concatenate([paired[:, 0], paired[:, 1]], axis=2)  8.61 us
    select_n x3, other arithmetic, target_levels(): upper_part = jnp.where(is_upper, state, partner)  7.55 us
  transfers between devices with their start and end apart: 3, of which 3 were waited for; matrix products, arithmetic and copies ran while one was open for 3% of the time, Pallas kernels for 0%

commit v1 on v0

v1 whole, which is shorter than its diff:
```python
import functools

import jax
import jax.numpy as jnp
from jax import lax
from jax.experimental import pallas as pl
from jax.experimental.pallas import tpu as pltpu
from jax.sharding import PartitionSpec as P


CHUNKS = (128, 128, 128, 128)
SHIFTS = (1, 3, 2)
VMEM_LIMIT = 8 * 1024 * 1024


def pack_pair(first, second):
    real = jnp.concatenate([first[0], second[0]], axis=0)
    imag = jnp.concatenate([first[1], second[1]], axis=0)
    return jnp.concatenate([real, imag], axis=1)


def block_product(blocks, packed):
    count, _, rank, wide = blocks.shape
    cols = packed.shape[1] // 2
    terms = jnp.dot(
        blocks.reshape(count * 2 * rank, wide), packed, preferred_element_type=jnp.float32
    )
    results = []
    for idx in range(count):
        top = terms[2 * idx * rank : (2 * idx + 1) * rank]
        low = terms[(2 * idx + 1) * rank : (2 * idx + 2) * rank]
        real = top[:, :cols] - low[:, cols:]
        imag = top[:, cols:] + low[:, :cols]
        results.append((real.astype(jnp.bfloat16), imag.astype(jnp.bfloat16)))
    return results


def source_kernel(first_col, order_ref, boxes_ref, blocks_ref, out_ref, middle):
    cols = out_ref.shape[-1]
    count = out_ref.shape[0]
    columns = pl.ds(first_col, cols)
    for level in range(2):
        write = out_ref if level else middle

        def step(pair, _, level=level, write=write):
            base = 2 * pair
            ids = order_ref[level, base], order_ref[level, base + 1]
            if level:
                boxes = [middle[idx] for idx in ids]
            else:
                boxes = [boxes_ref[idx, :, :, columns] for idx in ids]
            packed = pack_pair(*boxes)
            pairs = block_product(blocks_ref[level, pl.ds(base, 2)], packed)
            for idx, (real, imag) in enumerate(pairs):
                write[base + idx, 0] = real
                write[base + idx, 1] = imag
            return 0

        lax.fori_loop(0, count // 2, step, 0, unroll=2)


IN_VMEM = pl.BlockSpec(memory_space=pltpu.VMEM)
IN_SMEM = pl.BlockSpec(memory_space=pltpu.SMEM)


def source_levels(boxes, blocks, order, first_col, cols):
    count, _, rank, _ = boxes.shape
    shape = (count, 2, rank, cols)
    return pl.pallas_call(
        functools.partial(source_kernel, first_col),
        out_shape=jax.ShapeDtypeStruct(shape, jnp.bfloat16),
        in_specs=[IN_SMEM, IN_VMEM, IN_VMEM],
        out_specs=IN_VMEM,
        scratch_shapes=[pltpu.VMEM(shape, jnp.bfloat16)],
        compiler_params=pltpu.CompilerParams(vmem_limit_bytes=VMEM_LIMIT),
        name="source_levels",
    )(order, boxes, blocks)


def core_kernel(place_ref, own_ref, other_ref, blocks_ref, *out_refs):
    row = place_ref[0]
    is_upper = place_ref[1] == 1
    part = out_refs[0].shape[0]
    for shift, out_ref in enumerate(out_refs):
        base = ((row + shift) & 3) * part
        for idx in range(part):
            own, other = own_ref[base + idx], other_ref[base + idx]
            lower = jnp.where(is_upper, other, own)
            upper = jnp.where(is_upper, own, other)
            ((real, imag),) = block_product(
                blocks_ref[pl.ds(base + idx, 1)], pack_pair(lower, upper)
            )
            out_ref[idx, 0] = real
            out_ref[idx, 1] = imag


def core_level(place, own, other, blocks):
    count, _, rank, cols = own.shape
    return pl.pallas_call(
        core_kernel,
        out_shape=[jax.ShapeDtypeStruct((count // 4, 2, rank, cols), jnp.bfloat16)] * 4,
        in_specs=[IN_SMEM, IN_VMEM, IN_VMEM, IN_VMEM],
        out_specs=[IN_VMEM] * 4,
        compiler_params=pltpu.CompilerParams(vmem_limit_bytes=VMEM_LIMIT),
        name="core_level",
    )(place, own, other, blocks)


def slice_kernel(place_ref, blocks_ref, *refs):
    out_refs, sem = refs[:-1], refs[-1]
    row = place_ref[0]
    part = out_refs[0].shape[1]
    copies = []
    for shift, out_ref in enumerate(out_refs):
        start = ((row + shift) & 3) * part
        for level in range(2):
            view = blocks_ref.at[1 + level, pl.ds(start, part)]
            copies.append(
                pltpu.make_async_copy(view, out_ref.at[level], sem.at[shift, level])
            )
            copies[-1].start()
    for copy in copies:
        copy.wait()


def slice_blocks(place, blocks):
    _, count, _, rank, wide = blocks.shape
    shape = (2, count // 4, 2, rank, wide)
    return pl.pallas_call(
        slice_kernel,
        out_shape=[jax.ShapeDtypeStruct(shape, jnp.bfloat16)] * 4,
        in_specs=[IN_SMEM, pl.BlockSpec(memory_space=pltpu.HBM)],
        out_specs=[IN_VMEM] * 4,
        scratch_shapes=[pltpu.SemaphoreType.DMA((4, 2))],
        compiler_params=pltpu.CompilerParams(vmem_limit_bytes=VMEM_LIMIT),
        name="slice_blocks",
    )(place, blocks)


def plane_kernel(place_ref, x0, x1, x2, x3, w0, w1, w2, w3, o0, o1, o2, o3, middle):
    row = place_ref[0]
    part = x0.shape[0]
    states, blocks, outs = (x0, x1, x2, x3), (w0, w1, w2, w3), (o0, o3, o2, o1)

    def pair_blocks(level, first, second, idx):
        return jnp.concatenate(
            [blocks[first][level, pl.ds(idx, 1)], blocks[second][level, pl.ds(idx, 1)]], axis=0
        )

    def first_level(pairs):
        def step(idx, _):
            for low, high in pairs:
                packed = pack_pair(states[low][idx], states[high][idx])
                results = block_product(pair_blocks(0, low, high, idx), packed)
                for source, (real, imag) in zip((low, high), results):
                    plane = (row + 4 - source) & 3
                    middle[plane, idx, 0] = real
                    middle[plane, idx, 1] = imag
            return 0

        lax.fori_loop(0, part, step, 0)

    @pl.when((row & 1) == 0)
    def _():
        first_level(((0, 3), (2, 1)))

    @pl.when((row & 1) == 1)
    def _():
        first_level(((1, 0), (3, 2)))

    def step(idx, _):
        for source in range(2):
            plane = (row + 4 - source) & 1
            packed = pack_pair(middle[plane, idx], middle[plane + 2, idx])
            results = block_product(pair_blocks(1, source, source + 2, idx), packed)
            for target, (real, imag) in zip((source, source + 2), results):
                outs[target][idx, 0] = real
                outs[target][idx, 1] = imag
        return 0

    lax.fori_loop(0, part, step, 0)


def plane_levels(place, states, blocks):
    part, _, rank, cols = states[0].shape
    return pl.pallas_call(
        plane_kernel,
        out_shape=[jax.ShapeDtypeStruct((part, 2, rank, cols), jnp.bfloat16)] * 4,
        in_specs=[IN_SMEM] + [IN_VMEM] * 8,
        out_specs=[IN_VMEM] * 4,
        scratch_shapes=[pltpu.VMEM((4, part, 2, rank, cols), jnp.bfloat16)],
        compiler_params=pltpu.CompilerParams(vmem_limit_bytes=VMEM_LIMIT),
        name="plane_levels",
    )(place, *states, *blocks)


def place_kernel(chunk_cols, place_ref, *refs):
    pieces, out_ref, sem = refs[:-2], refs[-2], refs[-1]
    row = place_ref[0]
    part = pieces[0].shape[0]
    copies = []
    for idx, piece in enumerate(pieces):
        chunk, shift = divmod(idx, 4)
        slot = (row + 4 - shift) & 3
        columns = pl.ds(sum(chunk_cols[:chunk]), chunk_cols[chunk])
        view = out_ref.at[pl.ds(slot * part, part), :, :, columns]
        copies.append(pltpu.make_async_copy(piece, view, sem.at[idx]))
        copies[-1].start()
    for copy in copies:
        copy.wait()


def put_together(place, pieces, chunk_cols):
    part, _, rank, _ = pieces[0].shape
    return pl.pallas_call(
        functools.partial(place_kernel, chunk_cols),
        out_shape=jax.ShapeDtypeStruct((4 * part, 2, rank, sum(chunk_cols)), jnp.bfloat16),
        in_specs=[IN_SMEM] + [IN_VMEM] * len(pieces),
        out_specs=pl.BlockSpec(memory_space=pltpu.HBM),
        scratch_shapes=[pltpu.SemaphoreType.DMA((len(pieces),))],
        compiler_params=pltpu.CompilerParams(vmem_limit_bytes=VMEM_LIMIT),
        name="put_together",
    )(place, *pieces)


def along_y(value, shift):
    size = lax.axis_size("grp")
    pairs = [(g, (g + 2 * shift) % size) for g in range(size)]
    return lax.ppermute(value, "grp", pairs)


def other_core(value):
    return lax.ppermute(value, "grp", [(g, g ^ 1) for g in range(lax.axis_size("grp"))])


def on_device(coefficients, source_blocks, target_blocks, pair_tables):
    group = lax.axis_index("grp")
    row, core = group >> 1, group & 1
    place = jnp.stack([row, core]).astype(jnp.int32)
    order = pair_tables.reshape(pair_tables.shape[0], pair_tables.shape[2])

    first_blocks = target_blocks[0]
    own_blocks = slice_blocks(place, target_blocks)
    moved = {shift: along_y(own_blocks[shift], shift) for shift in SHIFTS}
    blocks = [own_blocks[0], moved[1], moved[2], moved[3]]

    pieces = []
    for chunk, cols in enumerate(CHUNKS):
        state = source_levels(coefficients, source_blocks, order, sum(CHUNKS[:chunk]), cols)
        state = lax.all_to_all(state, "wide", split_axis=0, concat_axis=0, tiled=True)
        other = other_core(state)
        outs = core_level(place, state, other, first_blocks)
        arrived = {shift: along_y(outs[shift], shift) for shift in SHIFTS}
        states = [outs[0], arrived[1], arrived[2], arrived[3]]
        results = plane_levels(place, states, blocks)
        home = {shift: along_y(results[shift], shift) for shift in SHIFTS}
        pieces += [results[0], home[1], home[2], home[3]]
    return put_together(place, pieces, CHUNKS)


def solution(mesh):
    in_specs = (
        P(("grp", "wide"), None, None, None),
        P(None, ("grp", "wide"), None, None, None),
        P(None, ("grp", "wide"), None, None, None),
        P(None, ("grp", "wide"), None),
    )
    out_specs = P(("grp", "wide"), None, None, None)

    return jax.shard_map(
        on_device, mesh=mesh, in_specs=in_specs, out_specs=out_specs, check_vma=False
    )
```

time: 363 us -> 229 us (0.63)
  waiting for transfers between devices: 180 us -> 102 us
  blocking collectives: 58.8 us -> 0 us
  starting transfers between devices: 4.77 us -> 57.8 us
  Pallas kernels: 0 us -> 45.3 us
  local copies, waits for them, and re-layouts: 60.6 us -> 22.7 us
  matrix products: 30.6 us -> 0 us
  other arithmetic: 26.8 us -> 0.08 us
    ppermute x3 -> x31, waiting for transfers between devices: 180 us -> 75.3 us  [the longest x27 75.3 us: along_y(): return lax.ppermute(value, 'grp', pairs)]
    all_to_all x1 -> x0, blocking collectives: 58.8 us -> none  [on_device(): lax.all_to_all(current, 'wide', split_axis=0, concat_axis=0, tiled=True)]
    pallas_call x0 -> x14, Pallas kernels: none -> 45.3 us  [the longest x4 15.8 us: source_levels(): pl.pallas_call(functools.partial(source_kernel, first_col), out_shape=jax...]
    ppermute x3 -> x31, starting transfers between devices: 4.77 us -> 36.7 us  [the longest x27 36.1 us: along_y(): return lax.ppermute(value, 'grp', pairs)]
    dot_general x20 -> x0, matrix products: 30.6 us -> none  [the longest x5 10.9 us: complex_terms(): jnp.einsum('nij,njk->nik', blocks[:, 0], stacked[:, 0], preferred_element...]
    all_to_all x0 -> x4, waiting for transfers between devices: none -> 26.2 us  [on_device(): lax.all_to_all(state, 'wide', split_axis=0, concat_axis=0, tiled=True)]
    all_to_all x0 -> x4, starting transfers between devices: none -> 21.1 us  [on_device(): lax.all_to_all(state, 'wide', split_axis=0, concat_axis=0, tiled=True)]
    unnamed x17 -> x20, local copies, waits for them, and re-layouts: 6.35 us -> 21 us
  transfers between devices with their start and end apart: 3 -> 35, of which waited for: 3 -> 22; matrix products, arithmetic and copies ran while one was open for 3% -> 1% of each run, Pallas kernels for 0% -> 17%
where the time goes in v1:
time: 229 us; the launch traced here: 228 us
  waiting for transfers between devices  102 us (45%)
  starting transfers between devices  57.8 us (25%)
  Pallas kernels  45.3 us (20%)
  local copies, waits for them, and re-layouts  22.7 us (10%)
    ppermute x27, waiting for transfers between devices, along_y(): return lax.ppermute(value, 'grp', pairs)  75.3 us
    ppermute x27, starting transfers between devices, along_y(): return lax.ppermute(value, 'grp', pairs)  36.1 us
    all_to_all x4, waiting for transfers between devices, on_device(): lax.all_to_all(state, 'wide', split_axis=0, concat_axis=0, tiled=True)  26.2 us
    all_to_all x4, starting transfers between devices, on_device(): lax.all_to_all(state, 'wide', split_axis=0, concat_axis=0, tiled=True)  21.1 us
    unnamed x20, local copies, waits for them, and re-layouts  21 us
    pallas_call x4, Pallas kernels, source_levels(): pl.pallas_call(functools.partial(source_kernel, first_col), out_shape=jax...  15.8 us
    pallas_call x4, Pallas kernels, plane_levels(): pl.pallas_call(plane_kernel, out_shape=[jax.ShapeDtypeStruct((part, 2, ra...  14.7 us
    pallas_call x4, Pallas kernels, core_level(): pl.pallas_call(core_kernel, out_shape=[jax.ShapeDtypeStruct((count // 4,...  9.52 us
  transfers between devices with their start and end apart: 35, of which 22 were waited for; matrix products, arithmetic and copies ran while one was open for 1% of the time, Pallas kernels for 17%

profile of v1, /device:TPU:0, one launch (start us, length us, event | category | flops | bytes accessed | tf_op | source)
XLA Modules:
  0.0 227.7 jit_solution(5877397240316384566)
XLA Ops:
  5.1 3.9 %source_levels.6 = bf16[16,2,128,128]{3,2,1,0:T(8,128)(2,1)} custom-call(s32[2,16]{1,0:T(2,128)S(1)} %bitcast.5, bf16[16,2,128,512]{3,2,1,0:T(8,128)(2,1)S(1)} %copy-done, bf16[2,16,2,128,256]{4,3,2,1,0:T(8,128)(2,1)S(1)} %copy-done.4), custom_call_target="tpu_custom_call" | custom-call | tf_op jit(solution)/shard_map/source_levels/pallas_call | solution.py:69
  9.0 8.0 %all-to-all-start.2 = ((bf16[16,2,128,128]{3,2,1,0:T(8,128)(2,1)}), bf16[16,2,128,128]{3,2,1,0:T(8,128)(2,1)}, u32[]{:S(2)}, u32[]{:S(2)}) async-start(bf16[16,2,128,128]{3,2,1,0:T(8,128)(2,1)} %source_levels.6), calls=%async_computation.2 | async-start | bytes 2097152 | tf_op jit(solution)/shard_map/all_to_all | solution.py:250
  21.4 4.0 %source_levels.5 = bf16[16,2,128,128]{3,2,1,0:T(8,128)(2,1)} custom-call(s32[2,16]{1,0:T(2,128)S(1)} %bitcast.6, bf16[16,2,128,512]{3,2,1,0:T(8,128)(2,1)S(1)} %copy-done.1, bf16[2,16,2,128,256]{4,3,2,1,0:T(8,128)(2,1)S(1)} %copy-done.5), custom_call_target="tpu_custom_call" | custom-call | tf_op jit(solution)/shard_map/source_levels/pallas_call | solution.py:69
  25.4 9.4 %all-to-all-done.2.own_ref = bf16[16,2,128,128]{3,2,1,0:T(8,128)(2,1)} async-done(((bf16[16,2,128,128]{3,2,1,0:T(8,128)(2,1)}), bf16[16,2,128,128]{3,2,1,0:T(8,128)(2,1)}, u32[]{:S(2)}, u32[]{:S(2)}) %all-to-all-start.2) | async-done | bytes 1048608 | tf_op jit(solution)/shard_map/all_to_all | solution.py:250
  34.8 4.3 %all-to-all-start.1 = ((bf16[16,2,128,128]{3,2,1,0:T(8,128)(2,1)}), bf16[16,2,128,128]{3,2,1,0:T(8,128)(2,1)}, u32[]{:S(2)}, u32[]{:S(2)}) async-start(bf16[16,2,128,128]{3,2,1,0:T(8,128)(2,1)} %source_levels.5), calls=%async_computation.1 | async-start | bytes 2097152 | tf_op jit(solution)/shard_map/all_to_all | solution.py:250
  43.5 3.9 %source_levels.4 = bf16[16,2,128,128]{3,2,1,0:T(8,128)(2,1)} custom-call(s32[2,16]{1,0:T(2,128)S(1)} %bitcast.7, bf16[16,2,128,512]{3,2,1,0:T(8,128)(2,1)S(1)} %copy-done.2, bf16[2,16,2,128,256]{4,3,2,1,0:T(8,128)(2,1)S(1)} %copy-done.6), custom_call_target="tpu_custom_call" | custom-call | tf_op jit(solution)/shard_map/source_levels/pallas_call | solution.py:69
  47.5 7.6 %all-to-all-done.1.own_ref = bf16[16,2,128,128]{3,2,1,0:T(8,128)(2,1)} async-done(((bf16[16,2,128,128]{3,2,1,0:T(8,128)(2,1)}), bf16[16,2,128,128]{3,2,1,0:T(8,128)(2,1)}, u32[]{:S(2)}, u32[]{:S(2)}) %all-to-all-start.1) | async-done | bytes 1048608 | tf_op jit(solution)/shard_map/all_to_all | solution.py:250
  55.0 4.4 %all-to-all-start = ((bf16[16,2,128,128]{3,2,1,0:T(8,128)(2,1)}), bf16[16,2,128,128]{3,2,1,0:T(8,128)(2,1)}, u32[]{:S(2)}, u32[]{:S(2)}) async-start(bf16[16,2,128,128]{3,2,1,0:T(8,128)(2,1)} %source_levels.4), calls=%async_computation | async-start | bytes 2097152 | tf_op jit(solution)/shard_map/all_to_all | solution.py:250
  64.4 3.9 %source_levels.7 = bf16[16,2,128,128]{3,2,1,0:T(8,128)(2,1)} custom-call(s32[2,16]{1,0:T(2,128)S(1)} %bitcast.8, bf16[16,2,128,512]{3,2,1,0:T(8,128)(2,1)S(1)} %copy-done.3, bf16[2,16,2,128,256]{4,3,2,1,0:T(8,128)(2,1)S(1)} %copy-done.7), custom_call_target="tpu_custom_call" | custom-call | tf_op jit(solution)/shard_map/source_levels/pallas_call | solution.py:69
  68.3 6.1 %all-to-all-done.own_ref = bf16[16,2,128,128]{3,2,1,0:T(8,128)(2,1)} async-done(((bf16[16,2,128,128]{3,2,1,0:T(8,128)(2,1)}), bf16[16,2,128,128]{3,2,1,0:T(8,128)(2,1)}, u32[]{:S(2)}, u32[]{:S(2)}) %all-to-all-start) | async-done | bytes 1048608 | tf_op jit(solution)/shard_map/all_to_all | solution.py:250
  74.4 4.3 %all-to-all-start.3 = ((bf16[16,2,128,128]{3,2,1,0:T(8,128)(2,1)}), bf16[16,2,128,128]{3,2,1,0:T(8,128)(2,1)}, u32[]{:S(2)}, u32[]{:S(2)}) async-start(bf16[16,2,128,128]{3,2,1,0:T(8,128)(2,1)} %source_levels.7), calls=%async_computation.3 | async-start | bytes 2097152 | tf_op jit(solution)/shard_map/all_to_all | solution.py:250
  78.8 2.8 %copy-done.8 = bf16[3,16,2,128,256]{4,3,2,1,0:T(8,128)(2,1)S(1)} copy-done((bf16[3,16,2,128,256]{4,3,2,1,0:T(8,128)(2,1)S(1)}, bf16[3,16,2,128,256]{4,3,2,1,0:T(8,128)(2,1)}, u32[]{:S(2)}) %copy-start.8) | copy-done | bytes 6291480
  81.6 2.6 %slice_blocks.1 = (bf16[2,4,2,128,256]{4,3,2,1,0:T(8,128)(2,1)S(1)}, bf16[2,4,2,128,256]{4,3,2,1,0:T(8,128)(2,1)}, bf16[2,4,2,128,256]{4,3,2,1,0:T(8,128)(2,1)}, bf16[2,4,2,128,256]{4,3,2,1,0:T(8,128)(2,1)}) custom-call(s32[2]{0:T(128)S(1)} %pad_add_fusion.place_ref, bf16[3,16,2,128,256]{4,3,2,1,0:T(8,128)(2,1)S(1)} %copy-done.8), custom_call_target="tpu_custom_call" | custom-call | tf_op jit(solution)/shard_map/slice_blocks/pallas_call | solution.py:129
  85.8 2.9 %collective-permute-start.5 = (bf16[2,4,2,128,256]{4,3,2,1,0:T(8,128)(2,1)}, bf16[2,4,2,128,256]{4,3,2,1,0:T(8,128)(2,1)S(1)}, u32[]{:S(2)}, u32[]{:S(2)}) collective-permute-start(bf16[2,4,2,128,256]{4,3,2,1,0:T(8,128)(2,1)} %get-tuple-element.47), channel_id=1, source_target_pairs={{0,64},{16,80},{32,96},{48,112},{64,0},{80,16},{96,32},{112,48},{1... | collective-permute-start | bytes 3145736 | tf_op jit(solution)/shard_map/ppermute | solution.py:229
  90.1 3.2 %all-to-all-done.3.own_ref = bf16[16,2,128,128]{3,2,1,0:T(8,128)(2,1)} async-done(((bf16[16,2,128,128]{3,2,1,0:T(8,128)(2,1)}), bf16[16,2,128,128]{3,2,1,0:T(8,128)(2,1)}, u32[]{:S(2)}, u32[]{:S(2)}) %all-to-all-start.3) | async-done | bytes 1048608 | tf_op jit(solution)/shard_map/all_to_all | solution.py:250
  100.0 27.9 %collective-permute-done.4.w1 = bf16[2,4,2,128,256]{4,3,2,1,0:T(8,128)(2,1)S(1)} collective-permute-done((bf16[2,4,2,128,256]{4,3,2,1,0:T(8,128)(2,1)}, bf16[2,4,2,128,256]{4,3,2,1,0:T(8,128)(2,1)S(1)}, u32[]{:S(2)}, u32[]{:S(2)}) %collective-permute-start.4) | collective-permute-done | bytes 1048608 | tf_op jit(solution)/shard_map/ppermute | solution.py:229
  127.8 2.8 %collective-permute-start.18 = (bf16[4,2,128,128]{3,2,1,0:T(8,128)(2,1)S(1)}, bf16[4,2,128,128]{3,2,1,0:T(8,128)(2,1)S(1)}, u32[]{:S(2)}, u32[]{:S(2)}) collective-permute-start(bf16[4,2,128,128]{3,2,1,0:T(8,128)(2,1)S(1)} %get-tuple-element.62), channel_id=1, source_target_pairs={{0,32},{16,48},{32,64},{48,80},{64,96},{80,112},{96,0},{112,16},{1... | collective-permute-start | bytes 786440 | tf_op jit(solution)/shard_map/ppermute | solution.py:229
  130.6 4.9 %collective-permute-done.5.w2 = bf16[2,4,2,128,256]{4,3,2,1,0:T(8,128)(2,1)S(1)} collective-permute-done((bf16[2,4,2,128,256]{4,3,2,1,0:T(8,128)(2,1)}, bf16[2,4,2,128,256]{4,3,2,1,0:T(8,128)(2,1)S(1)}, u32[]{:S(2)}, u32[]{:S(2)}) %collective-permute-start.5) | collective-permute-done | bytes 1048608 | tf_op jit(solution)/shard_map/ppermute | solution.py:229
  136.1 2.7 %collective-permute-start.13 = (bf16[4,2,128,128]{3,2,1,0:T(8,128)(2,1)S(1)}, bf16[4,2,128,128]{3,2,1,0:T(8,128)(2,1)S(1)}, u32[]{:S(2)}, u32[]{:S(2)}) collective-permute-start(bf16[4,2,128,128]{3,2,1,0:T(8,128)(2,1)S(1)} %get-tuple-element.56), channel_id=1, source_target_pairs={{0,96},{16,112},{32,0},{48,16},{64,32},{80,48},{96,64},{112,80},{1... | collective-permute-start | bytes 786440 | tf_op jit(solution)/shard_map/ppermute | solution.py:229
  141.3 2.9 %collective-permute-start.19 = (bf16[4,2,128,128]{3,2,1,0:T(8,128)(2,1)S(1)}, bf16[4,2,128,128]{3,2,1,0:T(8,128)(2,1)S(1)}, u32[]{:S(2)}, u32[]{:S(2)}) collective-permute-start(bf16[4,2,128,128]{3,2,1,0:T(8,128)(2,1)S(1)} %get-tuple-element.63), channel_id=1, source_target_pairs={{0,64},{16,80},{32,96},{48,112},{64,0},{80,16},{96,32},{112,48},{1... | collective-permute-start | bytes 786440 | tf_op jit(solution)/shard_map/ppermute | solution.py:229
  144.8 6.8 %collective-permute-done.11.x1 = bf16[4,2,128,128]{3,2,1,0:T(8,128)(2,1)S(1)} collective-permute-done((bf16[4,2,128,128]{3,2,1,0:T(8,128)(2,1)S(1)}, bf16[4,2,128,128]{3,2,1,0:T(8,128)(2,1)S(1)}, u32[]{:S(2)}, u32[]{:S(2)}) %collective-permute-start.11) | collective-permute-done | bytes 262176 | tf_op jit(solution)/shard_map/ppermute | solution.py:229
  154.6 2.6 %collective-permute-start.3 = (bf16[4,2,128,128]{3,2,1,0:T(8,128)(2,1)S(1)}, bf16[4,2,128,128]{3,2,1,0:T(8,128)(2,1)S(1)}, u32[]{:S(2)}, u32[]{:S(2)}) collective-permute-start(bf16[4,2,128,128]{3,2,1,0:T(8,128)(2,1)S(1)} %get-tuple-element.44), channel_id=1, source_target_pairs={{0,96},{16,112},{32,0},{48,16},{64,32},{80,48},{96,64},{112,80},{1... | collective-permute-start | bytes 786440 | tf_op jit(solution)/shard_map/ppermute | solution.py:229
  159.4 3.7 %plane_levels.5 = (bf16[4,2,128,128]{3,2,1,0:T(8,128)(2,1)S(1)}, bf16[4,2,128,128]{3,2,1,0:T(8,128)(2,1)S(1)}, bf16[4,2,128,128]{3,2,1,0:T(8,128)(2,1)S(1)}, bf16[4,2,128,128]{3,2,1,0:T(8,128)(2,1)S(1)}) custom-call(s32[2]{0:T(128)S(1)} %pad_add_fusion.place_ref, bf16[4,2,128,128]{3,2,1,0:T(8,128)(2,1)S(1)} %get-tuple-element.53.x0, ...), custom_call_target="tpu_custom_call" | custom-call | tf_op jit(solution)/shard_map/plane_levels/pallas_call | solution.py:186
  169.4 5.5 %collective-permute-done.3.x3 = bf16[4,2,128,128]{3,2,1,0:T(8,128)(2,1)S(1)} collective-permute-done((bf16[4,2,128,128]{3,2,1,0:T(8,128)(2,1)S(1)}, bf16[4,2,128,128]{3,2,1,0:T(8,128)(2,1)S(1)}, u32[]{:S(2)}, u32[]{:S(2)}) %collective-permute-start.3) | collective-permute-done | bytes 262176 | tf_op jit(solution)/shard_map/ppermute | solution.py:229
  175.6 3.7 %plane_levels.6 = (bf16[4,2,128,128]{3,2,1,0:T(8,128)(2,1)S(1)}, bf16[4,2,128,128]{3,2,1,0:T(8,128)(2,1)S(1)}, bf16[4,2,128,128]{3,2,1,0:T(8,128)(2,1)S(1)}, bf16[4,2,128,128]{3,2,1,0:T(8,128)(2,1)S(1)}) custom-call(s32[2]{0:T(128)S(1)} %pad_add_fusion.place_ref, bf16[4,2,128,128]{3,2,1,0:T(8,128)(2,1)S(1)} %get-tuple-element.61.x0, ...), custom_call_target="tpu_custom_call" | custom-call | tf_op jit(solution)/shard_map/plane_levels/pallas_call | solution.py:186
  179.2 3.7 %plane_levels.4 = (bf16[4,2,128,128]{3,2,1,0:T(8,128)(2,1)S(1)}, bf16[4,2,128,128]{3,2,1,0:T(8,128)(2,1)S(1)}, bf16[4,2,128,128]{3,2,1,0:T(8,128)(2,1)S(1)}, bf16[4,2,128,128]{3,2,1,0:T(8,128)(2,1)S(1)}) custom-call(s32[2]{0:T(128)S(1)} %pad_add_fusion.place_ref, bf16[4,2,128,128]{3,2,1,0:T(8,128)(2,1)S(1)} %get-tuple-element.41.x0, ...), custom_call_target="tpu_custom_call" | custom-call | tf_op jit(solution)/shard_map/plane_levels/pallas_call | solution.py:186
  192.0 3.7 %plane_levels.7 = (bf16[4,2,128,128]{3,2,1,0:T(8,128)(2,1)S(1)}, bf16[4,2,128,128]{3,2,1,0:T(8,128)(2,1)S(1)}, bf16[4,2,128,128]{3,2,1,0:T(8,128)(2,1)S(1)}, bf16[4,2,128,128]{3,2,1,0:T(8,128)(2,1)S(1)}) custom-call(s32[2]{0:T(128)S(1)} %pad_add_fusion.place_ref, bf16[4,2,128,128]{3,2,1,0:T(8,128)(2,1)S(1)} %get-tuple-element.69.x0, ...), custom_call_target="tpu_custom_call" | custom-call | tf_op jit(solution)/shard_map/plane_levels/pallas_call | solution.py:186
  203.2 5.5 %collective-permute-done.9.refs_3_ = bf16[4,2,128,128]{3,2,1,0:T(8,128)(2,1)S(1)} collective-permute-done((bf16[4,2,128,128]{3,2,1,0:T(8,128)(2,1)S(1)}, bf16[4,2,128,128]{3,2,1,0:T(8,128)(2,1)S(1)}, u32[]{:S(2)}, u32[]{:S(2)}) %collective-permute-start.9) | collective-permute-done | bytes 262176 | tf_op jit(solution)/shard_map/ppermute | solution.py:229
  211.9 2.5 %collective-permute-done.22.refs_10_ = bf16[4,2,128,128]{3,2,1,0:T(8,128)(2,1)S(1)} collective-permute-done((bf16[4,2,128,128]{3,2,1,0:T(8,128)(2,1)S(1)}, bf16[4,2,128,128]{3,2,1,0:T(8,128)(2,1)S(1)}, u32[]{:S(2)}, u32[]{:S(2)}) %collective-permute-start.22) | collective-permute-done | bytes 262176 | tf_op jit(solution)/shard_map/ppermute | solution.py:229
  214.4 4.8 %collective-permute-done.23.refs_11_ = bf16[4,2,128,128]{3,2,1,0:T(8,128)(2,1)S(1)} collective-permute-done((bf16[4,2,128,128]{3,2,1,0:T(8,128)(2,1)S(1)}, bf16[4,2,128,128]{3,2,1,0:T(8,128)(2,1)S(1)}, u32[]{:S(2)}, u32[]{:S(2)}) %collective-permute-start.23) | collective-permute-done | bytes 262176 | tf_op jit(solution)/shard_map/ppermute | solution.py:229
  221.1 3.8 %collective-permute-done.30.refs_15_ = bf16[4,2,128,128]{3,2,1,0:T(8,128)(2,1)S(1)} collective-permute-done((bf16[4,2,128,128]{3,2,1,0:T(8,128)(2,1)S(1)}, bf16[4,2,128,128]{3,2,1,0:T(8,128)(2,1)S(1)}, u32[]{:S(2)}, u32[]{:S(2)}) %collective-permute-start.30) | collective-permute-done | bytes 262176 | tf_op jit(solution)/shard_map/ppermute | solution.py:229
  224.9 2.7 %put_together.1 = bf16[16,2,128,512]{3,2,1,0:T(8,128)(2,1)} custom-call(s32[2]{0:T(128)S(1)} %pad_add_fusion.place_ref, bf16[4,2,128,128]{3,2,1,0:T(8,128)(2,1)S(1)} %get-tuple-element.49.refs_0_, bf16[4,2,128,128]{3,2,1,0:T(8,128)(2,1)S(1)} %collective-permute-done.7.refs_1_, bf16[4,2,128,128]{3,2,1,0:T(8,128)(2,1)S(1)} %collective-permute-done.8.refs_2_, ...), custom_call_target="tpu_custom_call" | custom-call | tf_op jit(solution)/shard_map/put_together/pallas_call | solution.py:215
  (74 shorter events, 65.9 us)
Async XLA Ops:
  9.0 25.8 %all-to-all-start.2 = ((bf16[16,2,128,128]{3,2,1,0:T(8,128)(2,1)}), bf16[16,2,128,128]{3,2,1,0:T(8,128)(2,1)}, u32[]{:S(2)}, u32[]{:S(2)}) async-start(bf16[16,2,128,128]{3,2,1,0:T(8,128)(2,1)} %source_levels.6), calls=%async_computation.2 | async-start | bytes 2097152 | tf_op jit(solution)/shard_map/all_to_all | solution.py:250
  34.8 20.3 %all-to-all-start.1 = ((bf16[16,2,128,128]{3,2,1,0:T(8,128)(2,1)}), bf16[16,2,128,128]{3,2,1,0:T(8,128)(2,1)}, u32[]{:S(2)}, u32[]{:S(2)}) async-start(bf16[16,2,128,128]{3,2,1,0:T(8,128)(2,1)} %source_levels.5), calls=%async_computation.1 | async-start | bytes 2097152 | tf_op jit(solution)/shard_map/all_to_all | solution.py:250
  55.0 19.3 %all-to-all-start = ((bf16[16,2,128,128]{3,2,1,0:T(8,128)(2,1)}), bf16[16,2,128,128]{3,2,1,0:T(8,128)(2,1)}, u32[]{:S(2)}, u32[]{:S(2)}) async-start(bf16[16,2,128,128]{3,2,1,0:T(8,128)(2,1)} %source_levels.4), calls=%async_computation | async-start | bytes 2097152 | tf_op jit(solution)/shard_map/all_to_all | solution.py:250
  59.4 30.7 %collective-permute-start.10 = (bf16[16,2,128,128]{3,2,1,0:T(8,128)(2,1)}, bf16[16,2,128,128]{3,2,1,0:T(8,128)(2,1)}, u32[]{:S(2)}, u32[]{:S(2)}) collective-permute-start(bf16[16,2,128,128]{3,2,1,0:T(8,128)(2,1)} %all-to-all-done.1.own_ref), channel_id=1, source_target_pairs={{0,16},{16,0},{32,48},{48,32},{64,80},{80,64},{96,112},{112,96},{1... | collective-permute-start | bytes 3145736 | tf_op jit(solution)/shard_map/ppermute | solution.py:233
  59.5 33.8 %collective-permute-start.17 = (bf16[16,2,128,128]{3,2,1,0:T(8,128)(2,1)}, bf16[16,2,128,128]{3,2,1,0:T(8,128)(2,1)}, u32[]{:S(2)}, u32[]{:S(2)}) collective-permute-start(bf16[16,2,128,128]{3,2,1,0:T(8,128)(2,1)} %all-to-all-done.2.own_ref), channel_id=1, source_target_pairs={{0,16},{16,0},{32,48},{48,32},{64,80},{80,64},{96,112},{112,96},{1... | collective-permute-start | bytes 3145736 | tf_op jit(solution)/shard_map/ppermute | solution.py:233
  74.4 18.9 %all-to-all-start.3 = ((bf16[16,2,128,128]{3,2,1,0:T(8,128)(2,1)}), bf16[16,2,128,128]{3,2,1,0:T(8,128)(2,1)}, u32[]{:S(2)}, u32[]{:S(2)}) async-start(bf16[16,2,128,128]{3,2,1,0:T(8,128)(2,1)} %source_levels.7), calls=%async_computation.3 | async-start | bytes 2097152 | tf_op jit(solution)/shard_map/all_to_all | solution.py:250
  84.2 43.7 %collective-permute-start.4 = (bf16[2,4,2,128,256]{4,3,2,1,0:T(8,128)(2,1)}, bf16[2,4,2,128,256]{4,3,2,1,0:T(8,128)(2,1)S(1)}, u32[]{:S(2)}, u32[]{:S(2)}) collective-permute-start(bf16[2,4,2,128,256]{4,3,2,1,0:T(8,128)(2,1)} %get-tuple-element.46), channel_id=1, source_target_pairs={{0,32},{16,48},{32,64},{48,80},{64,96},{80,112},{96,0},{112,16},{1... | collective-permute-start | bytes 3145736 | tf_op jit(solution)/shard_map/ppermute | solution.py:229
  85.8 49.6 %collective-permute-start.5 = (bf16[2,4,2,128,256]{4,3,2,1,0:T(8,128)(2,1)}, bf16[2,4,2,128,256]{4,3,2,1,0:T(8,128)(2,1)S(1)}, u32[]{:S(2)}, u32[]{:S(2)}) collective-permute-start(bf16[2,4,2,128,256]{4,3,2,1,0:T(8,128)(2,1)} %get-tuple-element.47), channel_id=1, source_target_pairs={{0,64},{16,80},{32,96},{48,112},{64,0},{80,16},{96,32},{112,48},{1... | collective-permute-start | bytes 3145736 | tf_op jit(solution)/shard_map/ppermute | solution.py:229
  88.7 46.7 %collective-permute-start.6 = (bf16[2,4,2,128,256]{4,3,2,1,0:T(8,128)(2,1)}, bf16[2,4,2,128,256]{4,3,2,1,0:T(8,128)(2,1)}, u32[]{:S(2)}, u32[]{:S(2)}) collective-permute-start(bf16[2,4,2,128,256]{4,3,2,1,0:T(8,128)(2,1)} %get-tuple-element.48), channel_id=1, source_target_pairs={{0,96},{16,112},{32,0},{48,16},{64,32},{80,48},{96,64},{112,80},{1... | collective-permute-start | bytes 3145736 | tf_op jit(solution)/shard_map/ppermute | solution.py:229
  90.1 46.0 %collective-permute-start = (bf16[16,2,128,128]{3,2,1,0:T(8,128)(2,1)}, bf16[16,2,128,128]{3,2,1,0:T(8,128)(2,1)}, u32[]{:S(2)}, u32[]{:S(2)}) collective-permute-start(bf16[16,2,128,128]{3,2,1,0:T(8,128)(2,1)} %all-to-all-done.own_ref), channel_id=1, source_target_pairs={{0,16},{16,0},{32,48},{48,32},{64,80},{80,64},{96,112},{112,96},{1... | collective-permute-start | bytes 3145736 | tf_op jit(solution)/shard_map/ppermute | solution.py:233
  93.3 48.0 %collective-permute-start.24 = (bf16[16,2,128,128]{3,2,1,0:T(8,128)(2,1)}, bf16[16,2,128,128]{3,2,1,0:T(8,128)(2,1)S(1)}, u32[]{:S(2)}, u32[]{:S(2)}) collective-permute-start(bf16[16,2,128,128]{3,2,1,0:T(8,128)(2,1)} %all-to-all-done.3.own_ref), channel_id=1, source_target_pairs={{0,16},{16,0},{32,48},{48,32},{64,80},{80,64},{96,112},{112,96},{1... | collective-permute-start | bytes 3145736 | tf_op jit(solution)/shard_map/ppermute | solution.py:233
  127.8 16.3 %collective-permute-start.18 = (bf16[4,2,128,128]{3,2,1,0:T(8,128)(2,1)S(1)}, bf16[4,2,128,128]{3,2,1,0:T(8,128)(2,1)S(1)}, u32[]{:S(2)}, u32[]{:S(2)}) collective-permute-start(bf16[4,2,128,128]{3,2,1,0:T(8,128)(2,1)S(1)} %get-tuple-element.62), channel_id=1, source_target_pairs={{0,32},{16,48},{32,64},{48,80},{64,96},{80,112},{96,0},{112,16},{1... | collective-permute-start | bytes 786440 | tf_op jit(solution)/shard_map/ppermute | solution.py:229
  135.5 16.2 %collective-permute-start.11 = (bf16[4,2,128,128]{3,2,1,0:T(8,128)(2,1)S(1)}, bf16[4,2,128,128]{3,2,1,0:T(8,128)(2,1)S(1)}, u32[]{:S(2)}, u32[]{:S(2)}) collective-permute-start(bf16[4,2,128,128]{3,2,1,0:T(8,128)(2,1)S(1)} %get-tuple-element.54), channel_id=1, source_target_pairs={{0,32},{16,48},{32,64},{48,80},{64,96},{80,112},{96,0},{112,16},{1... | collective-permute-start | bytes 786440 | tf_op jit(solution)/shard_map/ppermute | solution.py:229
  135.5 16.9 %collective-permute-start.12 = (bf16[4,2,128,128]{3,2,1,0:T(8,128)(2,1)S(1)}, bf16[4,2,128,128]{3,2,1,0:T(8,128)(2,1)S(1)}, u32[]{:S(2)}, u32[]{:S(2)}) collective-permute-start(bf16[4,2,128,128]{3,2,1,0:T(8,128)(2,1)S(1)} %get-tuple-element.55), channel_id=1, source_target_pairs={{0,64},{16,80},{32,96},{48,112},{64,0},{80,16},{96,32},{112,48},{1... | collective-permute-start | bytes 786440 | tf_op jit(solution)/shard_map/ppermute | solution.py:229
  136.1 18.5 %collective-permute-start.13 = (bf16[4,2,128,128]{3,2,1,0:T(8,128)(2,1)S(1)}, bf16[4,2,128,128]{3,2,1,0:T(8,128)(2,1)S(1)}, u32[]{:S(2)}, u32[]{:S(2)}) collective-permute-start(bf16[4,2,128,128]{3,2,1,0:T(8,128)(2,1)S(1)} %get-tuple-element.56), channel_id=1, source_target_pairs={{0,96},{16,112},{32,0},{48,16},{64,32},{80,48},{96,64},{112,80},{1... | collective-permute-start | bytes 786440 | tf_op jit(solution)/shard_map/ppermute | solution.py:229
  141.3 21.8 %collective-permute-start.19 = (bf16[4,2,128,128]{3,2,1,0:T(8,128)(2,1)S(1)}, bf16[4,2,128,128]{3,2,1,0:T(8,128)(2,1)S(1)}, u32[]{:S(2)}, u32[]{:S(2)}) collective-permute-start(bf16[4,2,128,128]{3,2,1,0:T(8,128)(2,1)S(1)} %get-tuple-element.63), channel_id=1, source_target_pairs={{0,64},{16,80},{32,96},{48,112},{64,0},{80,16},{96,32},{112,48},{1... | collective-permute-start | bytes 786440 | tf_op jit(solution)/shard_map/ppermute | solution.py:229
  144.2 19.5 %collective-permute-start.20 = (bf16[4,2,128,128]{3,2,1,0:T(8,128)(2,1)S(1)}, bf16[4,2,128,128]{3,2,1,0:T(8,128)(2,1)S(1)}, u32[]{:S(2)}, u32[]{:S(2)}) collective-permute-start(bf16[4,2,128,128]{3,2,1,0:T(8,128)(2,1)S(1)} %get-tuple-element.64), channel_id=1, source_target_pairs={{0,96},{16,112},{32,0},{48,16},{64,32},{80,48},{96,64},{112,80},{1... | collective-permute-start | bytes 786440 | tf_op jit(solution)/shard_map/ppermute | solution.py:229
  152.4 17.0 %collective-permute-start.2 = (bf16[4,2,128,128]{3,2,1,0:T(8,128)(2,1)S(1)}, bf16[4,2,128,128]{3,2,1,0:T(8,128)(2,1)S(1)}, u32[]{:S(2)}, u32[]{:S(2)}) collective-permute-start(bf16[4,2,128,128]{3,2,1,0:T(8,128)(2,1)S(1)} %get-tuple-element.43), channel_id=1, source_target_pairs={{0,64},{16,80},{32,96},{48,112},{64,0},{80,16},{96,32},{112,48},{1... | collective-permute-start | bytes 786440 | tf_op jit(solution)/shard_map/ppermute | solution.py:229
  154.6 20.3 %collective-permute-start.3 = (bf16[4,2,128,128]{3,2,1,0:T(8,128)(2,1)S(1)}, bf16[4,2,128,128]{3,2,1,0:T(8,128)(2,1)S(1)}, u32[]{:S(2)}, u32[]{:S(2)}) collective-permute-start(bf16[4,2,128,128]{3,2,1,0:T(8,128)(2,1)S(1)} %get-tuple-element.44), channel_id=1, source_target_pairs={{0,96},{16,112},{32,0},{48,16},{64,32},{80,48},{96,64},{112,80},{1... | collective-permute-start | bytes 786440 | tf_op jit(solution)/shard_map/ppermute | solution.py:229
  163.1 19.9 %collective-permute-start.25 = (bf16[4,2,128,128]{3,2,1,0:T(8,128)(2,1)S(1)}, bf16[4,2,128,128]{3,2,1,0:T(8,128)(2,1)S(1)}, u32[]{:S(2)}, u32[]{:S(2)}) collective-permute-start(bf16[4,2,128,128]{3,2,1,0:T(8,128)(2,1)S(1)} %get-tuple-element.70), channel_id=1, source_target_pairs={{0,32},{16,48},{32,64},{48,80},{64,96},{80,112},{96,0},{112,16},{1... | collective-permute-start | bytes 786440 | tf_op jit(solution)/shard_map/ppermute | solution.py:229
  163.6 21.5 %collective-permute-start.26 = (bf16[4,2,128,128]{3,2,1,0:T(8,128)(2,1)S(1)}, bf16[4,2,128,128]{3,2,1,0:T(8,128)(2,1)S(1)}, u32[]{:S(2)}, u32[]{:S(2)}) collective-permute-start(bf16[4,2,128,128]{3,2,1,0:T(8,128)(2,1)S(1)} %get-tuple-element.71), channel_id=1, source_target_pairs={{0,64},{16,80},{32,96},{48,112},{64,0},{80,16},{96,32},{112,48},{1... | collective-permute-start | bytes 786440 | tf_op jit(solution)/shard_map/ppermute | solution.py:229
  165.8 20.4 %collective-permute-start.27 = (bf16[4,2,128,128]{3,2,1,0:T(8,128)(2,1)S(1)}, bf16[4,2,128,128]{3,2,1,0:T(8,128)(2,1)S(1)}, u32[]{:S(2)}, u32[]{:S(2)}) collective-permute-start(bf16[4,2,128,128]{3,2,1,0:T(8,128)(2,1)S(1)} %get-tuple-element.72), channel_id=1, source_target_pairs={{0,96},{16,112},{32,0},{48,16},{64,32},{80,48},{96,64},{112,80},{1... | collective-permute-start | bytes 786440 | tf_op jit(solution)/shard_map/ppermute | solution.py:229
  169.3 18.6 %collective-permute-start.14 = (bf16[4,2,128,128]{3,2,1,0:T(8,128)(2,1)S(1)}, bf16[4,2,128,128]{3,2,1,0:T(8,128)(2,1)S(1)}, u32[]{:S(2)}, u32[]{:S(2)}) collective-permute-start(bf16[4,2,128,128]{3,2,1,0:T(8,128)(2,1)S(1)} %get-tuple-element.58), channel_id=1, source_target_pairs={{0,32},{16,48},{32,64},{48,80},{64,96},{80,112},{96,0},{112,16},{1... | collective-permute-start | bytes 786440 | tf_op jit(solution)/shard_map/ppermute | solution.py:229
  174.9 16.9 %collective-permute-start.15 = (bf16[4,2,128,128]{3,2,1,0:T(8,128)(2,1)S(1)}, bf16[4,2,128,128]{3,2,1,0:T(8,128)(2,1)S(1)}, u32[]{:S(2)}, u32[]{:S(2)}) collective-permute-start(bf16[4,2,128,128]{3,2,1,0:T(8,128)(2,1)S(1)} %get-tuple-element.59), channel_id=1, source_target_pairs={{0,64},{16,80},{32,96},{48,112},{64,0},{80,16},{96,32},{112,48},{1... | collective-permute-start | bytes 786440 | tf_op jit(solution)/shard_map/ppermute | solution.py:229
  185.1 14.6 %collective-permute-start.7 = (bf16[4,2,128,128]{3,2,1,0:T(8,128)(2,1)S(1)}, bf16[4,2,128,128]{3,2,1,0:T(8,128)(2,1)S(1)}, u32[]{:S(2)}, u32[]{:S(2)}) collective-permute-start(bf16[4,2,128,128]{3,2,1,0:T(8,128)(2,1)S(1)} %get-tuple-element.50), channel_id=1, source_target_pairs={{0,32},{16,48},{32,64},{48,80},{64,96},{80,112},{96,0},{112,16},{1... | collective-permute-start | bytes 786440 | tf_op jit(solution)/shard_map/ppermute | solution.py:229
  186.2 16.9 %collective-permute-start.8 = (bf16[4,2,128,128]{3,2,1,0:T(8,128)(2,1)S(1)}, bf16[4,2,128,128]{3,2,1,0:T(8,128)(2,1)S(1)}, u32[]{:S(2)}, u32[]{:S(2)}) collective-permute-start(bf16[4,2,128,128]{3,2,1,0:T(8,128)(2,1)S(1)} %get-tuple-element.51), channel_id=1, source_target_pairs={{0,64},{16,80},{32,96},{48,112},{64,0},{80,16},{96,32},{112,48},{1... | collective-permute-start | bytes 786440 | tf_op jit(solution)/shard_map/ppermute | solution.py:229
  187.9 20.8 %collective-permute-start.9 = (bf16[4,2,128,128]{3,2,1,0:T(8,128)(2,1)S(1)}, bf16[4,2,128,128]{3,2,1,0:T(8,128)(2,1)S(1)}, u32[]{:S(2)}, u32[]{:S(2)}) collective-permute-start(bf16[4,2,128,128]{3,2,1,0:T(8,128)(2,1)S(1)} %get-tuple-element.52), channel_id=1, source_target_pairs={{0,96},{16,112},{32,0},{48,16},{64,32},{80,48},{96,64},{112,80},{1... | collective-permute-start | bytes 786440 | tf_op jit(solution)/shard_map/ppermute | solution.py:229
  191.9 17.8 %collective-permute-start.21 = (bf16[4,2,128,128]{3,2,1,0:T(8,128)(2,1)S(1)}, bf16[4,2,128,128]{3,2,1,0:T(8,128)(2,1)S(1)}, u32[]{:S(2)}, u32[]{:S(2)}) collective-permute-start(bf16[4,2,128,128]{3,2,1,0:T(8,128)(2,1)S(1)} %get-tuple-element.66), channel_id=1, source_target_pairs={{0,32},{16,48},{32,64},{48,80},{64,96},{80,112},{96,0},{112,16},{1... | collective-permute-start | bytes 786440 | tf_op jit(solution)/shard_map/ppermute | solution.py:229
  197.5 16.9 %collective-permute-start.22 = (bf16[4,2,128,128]{3,2,1,0:T(8,128)(2,1)S(1)}, bf16[4,2,128,128]{3,2,1,0:T(8,128)(2,1)S(1)}, u32[]{:S(2)}, u32[]{:S(2)}) collective-permute-start(bf16[4,2,128,128]{3,2,1,0:T(8,128)(2,1)S(1)} %get-tuple-element.67), channel_id=1, source_target_pairs={{0,64},{16,80},{32,96},{48,112},{64,0},{80,16},{96,32},{112,48},{1... | collective-permute-start | bytes 786440 | tf_op jit(solution)/shard_map/ppermute | solution.py:229
  199.8 19.5 %collective-permute-start.23 = (bf16[4,2,128,128]{3,2,1,0:T(8,128)(2,1)S(1)}, bf16[4,2,128,128]{3,2,1,0:T(8,128)(2,1)S(1)}, u32[]{:S(2)}, u32[]{:S(2)}) collective-permute-start(bf16[4,2,128,128]{3,2,1,0:T(8,128)(2,1)S(1)} %get-tuple-element.68), channel_id=1, source_target_pairs={{0,96},{16,112},{32,0},{48,16},{64,32},{80,48},{96,64},{112,80},{1... | collective-permute-start | bytes 786440 | tf_op jit(solution)/shard_map/ppermute | solution.py:229
  203.1 16.1 %collective-permute-start.28 = (bf16[4,2,128,128]{3,2,1,0:T(8,128)(2,1)S(1)}, bf16[4,2,128,128]{3,2,1,0:T(8,128)(2,1)S(1)}, u32[]{:S(2)}, u32[]{:S(2)}) collective-permute-start(bf16[4,2,128,128]{3,2,1,0:T(8,128)(2,1)S(1)} %get-tuple-element.74), channel_id=1, source_target_pairs={{0,32},{16,48},{32,64},{48,80},{64,96},{80,112},{96,0},{112,16},{1... | collective-permute-start | bytes 786440 | tf_op jit(solution)/shard_map/ppermute | solution.py:229
  209.7 15.2 %collective-permute-start.30 = (bf16[4,2,128,128]{3,2,1,0:T(8,128)(2,1)S(1)}, bf16[4,2,128,128]{3,2,1,0:T(8,128)(2,1)S(1)}, u32[]{:S(2)}, u32[]{:S(2)}) collective-permute-start(bf16[4,2,128,128]{3,2,1,0:T(8,128)(2,1)S(1)} %get-tuple-element.76), channel_id=1, source_target_pairs={{0,96},{16,112},{32,0},{48,16},{64,32},{80,48},{96,64},{112,80},{1... | collective-permute-start | bytes 786440 | tf_op jit(solution)/shard_map/ppermute | solution.py:229
  (13 other events, 62.0 us)
